TPU v7x, 256 devices: a whole 4x4x8 slice. The times are simulated.
256 devices in a mesh: lat: 16 (over x, y), lon: 8 (over z), ens: 2 (over core).
Axes of the slice: x: 4, y: 4, z: 8, core: 2. Of those that a mesh axis runs over, the one named last changes fastest.
Arguments:
- parameters: float32 [2, 128, 128, 1024], P(None, 'ens', 'lat', 'lon'), may hold values from -1.2 to 1.2, as said below
- initial_height: float32 [128, 1024], P('lat', 'lon'), may hold values from -6 to 6
- initial_speed: float32 [2, 128, 1024], P(None, 'lat', 'lon'), may hold values from -4 to 4
- obs_slots: int32 [2, 128, 128, 8], P(None, ('lat', 'lon')), may hold values from -1 to 1023, as said below
- obs_values: float32 [2, 128, 128, 8], P(None, ('lat', 'lon')), may hold values from -6 to 6
- obs_precision: float32 [2, 128, 128, 8], P(None, ('lat', 'lon')), may hold values from 0 to 2, as said below
Outputs:
- calibrated: float32 [2, 128, 128, 1024], P(None, 'ens', 'lat', 'lon')
Inputs may be any that keep to these rules, and one draw needn't show every extreme that they name: `obs_slots`: for each iteration and owner, the live slots towards one receiver come first and name distinct cells of the owner's block (local index row * 128 + column); no cell is named twice by one owner in one iteration; in each iteration some receiving block has all 8 slots live from every owner. `obs_precision`: zero exactly where the matching slot of obs_slots (with receiver and owner swapped) is empty, 0.5 or more elsewhere. `parameters`: friction rates lie in 0.02 to 0.2, forcing in -1.2 to 1.2.
All inputs are finite; a program needn't handle non-finite values.
Results may differ from a plain program's by a relative error of at most 0.0003.
Values sent between devices are 32-bit elements; how exact they have to be, the bound alone decides.
No kernel may reach another device: no remote copies, remote signals or barrier semaphores. Data moves between devices by JAX's collectives and lax.ppermute only.
A program may use at most 64 MiB of HBM per device.

v0:
```python
import functools

import jax
import jax.numpy as jnp
from jax import lax
from jax.experimental import pallas as pl
from jax.experimental.pallas import tpu as pltpu
from jax.sharding import Mesh
from jax.sharding import PartitionSpec as P

STEPS = 6
LAT = ("lat_0", "lat_1")
LAT_LON = ("lat_0", "lat_1", "lon")
LON_ENS = ("lon", "ens")

DEPTH = 0.7
GRAVITY = 0.7
CORIOLIS = 0.1

MEMBERS = 128
HALF = 64
ROWS = 8
COLS = 128
EXT = 28
WIDE = 112
LEFT = 24
RIGHT = LEFT + HALF
INIT = 24
GLOBAL_ROWS = 128
OWN = 2 * ROWS * HALF
PIVOTS = 16

F32 = jnp.float32
HIGHEST = lax.Precision.HIGHEST
VMEM = pl.BlockSpec(memory_space=pltpu.VMEM)
SMEM = pl.BlockSpec(memory_space=pltpu.SMEM)


def params():
    return pltpu.CompilerParams(vmem_limit_bytes=24 * 1024 * 1024)


def shape(*dims):
    return jax.ShapeDtypeStruct(dims, F32)


def iota(dims, axis):
    return lax.broadcasted_iota(jnp.int32, dims, axis)


def spread_members(pos, own, other, height, speed, values, precision, out, up2, dn2, obs):
    def emit(low, high, first):
        for f in range(2):
            for r in range(ROWS):
                start = f * HALF * ROWS + r
                block = jnp.concatenate(
                    [low[pl.ds(start, HALF, stride=ROWS), :], high[pl.ds(start, HALF, stride=ROWS), :]],
                    axis=0,
                )
                turned = block.T[first : first + HALF]
                at = (f * ROWS + r) * HALF
                out[at : at + HALF] = turned
                if f == 1 and r >= 6:
                    up2[(r - 6) * HALF : (r - 5) * HALF] = turned
                if f == 0 and r == 7:
                    up2[2 * HALF : 3 * HALF] = turned
                if f == 1 and r < 2:
                    dn2[r * HALF : (r + 1) * HALF] = turned
                if f == 0 and r == 0:
                    dn2[2 * HALF : 3 * HALF] = turned

    for ref, at in ((out, OWN), (up2, 3 * HALF), (dn2, 3 * HALF)):
        ref[at : at + ROWS] = height[...]
        ref[at + ROWS : at + INIT] = speed[...]
    lines = [values[...], precision[...], jnp.zeros((96, MEMBERS), F32)]
    obs[...] = jnp.concatenate(lines, axis=0).T

    @pl.when(pos[1] == 0)
    def _():
        emit(own, other, 0)

    @pl.when(pos[1] == 1)
    def _():
        emit(other, own, HALF)


def edge_rows():
    rows = []
    for field, first in ((1, 0), (0, 1)):
        for r in range(first, EXT - first):
            away = max(10 - r, r - 17, 0)
            need = 9 + field - away
            rows.append((field, r, 16 if need > 8 else 8))
    return rows


EDGE_ROWS = edge_rows()
EDGE_FIELDS = sum(n for _, _, n in EDGE_ROWS)
EDGE = EDGE_FIELDS + 5 * INIT


def row_source(field, r, own, m1, p1, m2, p2):
    at = field * ROWS * HALF
    if 10 <= r < 18:
        return own, at + (r - 10) * HALF
    if 2 <= r < 10:
        return m1, at + (r - 2) * HALF
    if 18 <= r < 26:
        return p1, at + (r - 18) * HALF
    ref = m2 if r < 2 else p2
    if field == 1:
        return ref, (r if r < 2 else r - 26) * HALF
    return ref, 2 * HALF


def initial_tiles(own, m1, p1, m2, p2):
    return ((m2, 3 * HALF), (m1, OWN), (own, OWN), (p1, OWN), (p2, 3 * HALF))


def pack_edges(own, m1, p1, m2, p2, _, right, left):
    at = 0
    for field, r, n in EDGE_ROWS:
        ref, start = row_source(field, r, own, m1, p1, m2, p2)
        right[at : at + n] = ref[start + HALF - n : start + HALF]
        left[at : at + n] = ref[start : start + n]
        at += n
    for ref, start in initial_tiles(own, m1, p1, m2, p2):
        fields = ref[start : start + INIT]
        right[at : at + INIT] = fields
        left[at : at + INIT] = fields
        at += INIT


def scatter_obs(pos, slots, received, weights, observed):
    received = received[...].T
    values, precision = received[:16], received[16:32]
    lines = ROWS * HALF
    k = iota((lines, MEMBERS), 0)
    cell = (k // HALF) * COLS + pos[1] * HALF + k % HALF
    for t in range(2):
        found_w = jnp.zeros((lines, MEMBERS), F32)
        found_y = jnp.zeros((lines, MEMBERS), F32)
        for s in range(8):
            at = t * 8 + s
            hit = cell == slots[at : at + 1, :]
            found_w = found_w + jnp.where(hit, precision[at : at + 1, :], 0.0)
            found_y = found_y + jnp.where(hit, values[at : at + 1, :], 0.0)
        weights[t] = jnp.broadcast_to(jnp.sum(found_w, axis=1, keepdims=True), (lines, MEMBERS))
        observed[t] = jnp.broadcast_to(jnp.sum(found_y, axis=1, keepdims=True), (lines, MEMBERS))


def inside(lat, r):
    row = lat * ROWS + r - 10
    return jnp.logical_and(row >= 0, row < GLOBAL_ROWS)


def initial_table(pos, tiles, lz, rz):
    first = EDGE_FIELDS
    lane = iota((ROWS, COLS), 1)
    row = iota((ROWS, COLS), 0)
    e = pos[1]
    fields = [[], [], []]
    for k, (ref, start) in enumerate(tiles):
        for f in range(3):
            own = ref[start + f * ROWS : start + (f + 1) * ROWS]
            at = first + k * INIT + f * ROWS
            before = lz[at : at + ROWS]
            after = rz[at : at + ROWS]
            low = pltpu.roll(jnp.where(lane >= 112, before, own), 16, 1)
            high = pltpu.roll(jnp.where(lane < 16, after, own), 80, 1)
            window = jnp.where(e == 0, low, high)
            place = pos[0] * ROWS + (k - 2) * ROWS + row
            ok = jnp.logical_and(place >= 0, place < GLOBAL_ROWS)
            fields[f].append(jnp.where(ok, window, 0.0))
    h, u, v = (jnp.concatenate(f, axis=0) for f in fields)
    east = pltpu.roll(u, COLS - 1, 1) - pltpu.roll(u, 1, 1)
    north = jnp.concatenate([v[1:], v[:1]], axis=0) - jnp.concatenate([v[-1:], v[:-1]], axis=0)
    place = pos[0] * ROWS - 16 + iota((40, COLS), 0)
    ok = jnp.logical_and(place >= 0, place < GLOBAL_ROWS)
    base = jnp.where(ok, h - DEPTH * (east + north), 0.0)
    return jnp.concatenate([base, u, v, jnp.zeros((8, COLS), F32)], axis=0).T


def forward(lat, table, FR, FO, H, U, V):
    first = table[0:96]

    def start(f, r):
        lane = f * 40 + r + 6
        return jnp.broadcast_to(first[:, lane : lane + 1], (96, MEMBERS))

    def gains(r):
        ok = inside(lat, r)
        return jnp.where(ok, F32(GRAVITY), F32(0.0)), jnp.where(ok, F32(CORIOLIS), F32(0.0))

    for r in range(EXT):
        H[r, 8:104] = start(0, r) + FO[r, 8:104]
    for r in range(1, EXT - 1):
        g, c = gains(r)
        u, v = start(1, r), start(2, r)
        keep = 1.0 - FR[r, 8:104]
        U[r, 8:104] = keep * u - g * (H[r, 9:105] - H[r, 7:103]) + c * v
        V[r, 8:104] = keep * v - g * (H[r + 1, 8:104] - H[r - 1, 8:104]) - c * u

    def height_row(a, b, r):
        g, _ = gains(r)
        n = b - a
        east = U[r, pl.ds(a + 1, n)] - U[r, pl.ds(a - 1, n)]
        north = V[r + 1, pl.ds(a, n)] - V[r - 1, pl.ds(a, n)]
        H[r, pl.ds(a, n)] = H[r, pl.ds(a, n)] - g * (east + north) + FO[r, pl.ds(a, n)]

    def speed_row(a, b, r):
        g, c = gains(r)
        n = b - a
        u, v = U[r, pl.ds(a, n)], V[r, pl.ds(a, n)]
        keep = 1.0 - FR[r, pl.ds(a, n)]
        east = H[r, pl.ds(a + 1, n)] - H[r, pl.ds(a - 1, n)]
        north = H[r + 1, pl.ds(a, n)] - H[r - 1, pl.ds(a, n)]
        U[r, pl.ds(a, n)] = keep * u - g * east + c * v
        V[r, pl.ds(a, n)] = keep * v - g * north - c * u

    def sweep(row, reach, a, b):
        def body(i, carry):
            row(a, b, 10 - reach + 2 * i)
            row(a, b, 11 - reach + 2 * i)
            return carry

        lax.fori_loop(0, (ROWS + 2 * reach) // 2, body, 0)

    for step in range(1, STEPS):
        reach = 2 * (STEPS - 1 - step)
        a, b = (16, 96) if reach else (LEFT, RIGHT)
        sweep(height_row, reach, a, b)
        if reach:
            sweep(speed_row, reach - 1, a, b)


def gram(pos, H, weights, observed, keep, send):
    lines = ROWS * HALF
    h = H[10:18, LEFT:RIGHT].reshape(lines, MEMBERS)
    centre = jnp.mean(h, axis=1, keepdims=True)
    spread = h - centre
    weighted = spread * weights
    g = lax.dot_general(spread, weighted, (((0,), (0,)), ((), ())), precision=HIGHEST, preferred_element_type=F32)
    d = jnp.sum(weighted * (observed - centre), axis=0, keepdims=True)
    row, lane = iota((HALF, MEMBERS), 0), iota((HALF, MEMBERS), 1)
    top, bottom = g[:HALF], g[HALF:]
    packed = jnp.where(jnp.logical_and(lane < HALF, lane > row), pltpu.roll(bottom, HALF, 1), top)
    diagonal = jnp.sum(jnp.where(lane == row + HALF, bottom, 0.0), axis=0, keepdims=True)
    line = iota((8, MEMBERS), 0)
    rest = jnp.where(line == 0, d, jnp.where(line == 1, diagonal, 0.0))
    one = jnp.concatenate([packed[:32], rest], axis=0)
    two = jnp.concatenate([packed[32:], jnp.zeros((8, MEMBERS), F32)], axis=0)
    e = pos[1]
    keep[...] = jnp.where(e == 0, one, two)
    send[...] = jnp.where(e == 0, two, one)


def first_run(pos, own, m1, p1, m2, p2, lz, rz, weights, observed, FR, FO, table, keep, send, H, U, V):
    at = 0
    for field, r, n in EDGE_ROWS:
        ref, begin = row_source(field, r, own, m1, p1, m2, p2)
        west, middle, east = lz[at : at + n], ref[begin : begin + HALF], rz[at : at + n]
        at += n
        if field == 1 and not 10 <= r < 18:
            ok = inside(pos[0], r)
            west, middle, east = (jnp.where(ok, x, 0.0) for x in (west, middle, east))
        out = FO if field else FR
        out[r, LEFT - n : LEFT] = west
        out[r, LEFT:RIGHT] = middle
        out[r, RIGHT : RIGHT + n] = east
    table[...] = initial_table(pos, initial_tiles(own, m1, p1, m2, p2), lz, rz)
    forward(pos[0], table[...], FR, FO, H, U, V)
    gram(pos, H, weights[0], observed[0], keep, send)


def inverse(x):
    n = PIVOTS
    panels = [x[k : k + n] for k in range(0, MEMBERS, n)]
    row, lane = iota((n, MEMBERS), 0), iota((n, MEMBERS), 1)
    lower, scaled = [], []

    def spread(panel, column):
        return jnp.broadcast_to(panel[:, column : column + 1], (n, MEMBERS))

    for k in range(len(panels)):
        first = k * n
        block = jnp.logical_and(lane >= first, lane < first + n)
        columns = [spread(panels[k], first + j) for j in range(n)]
        top = jnp.where(block, jnp.where(lane - first == row, 1.0, 0.0), panels[k])
        lower.append(jnp.where(lane < first + n, top, 0.0))
        for j in range(n):
            over = 1.0 / columns[j][j : j + 1]

            def eliminate(m, j=j, over=over):
                pivot = m[j : j + 1] * over
                return jnp.where(row == j, pivot, m - columns[j] * pivot)

            top = eliminate(top)
            columns[j + 1 :] = [eliminate(m) for m in columns[j + 1 :]]
        scaled.append(jnp.where(lane < first + n, top, 0.0))
        for i in range(k + 1, len(panels)):
            terms = [spread(panels[i], first + j) * top[j : j + 1] for j in range(n)]
            while len(terms) > 1:
                terms = [a + b for a, b in zip(terms[::2], terms[1::2])]
            panels[i] = jnp.where(block, 0.0, panels[i]) - terms[0]
    lower, scaled = jnp.concatenate(lower, axis=0), jnp.concatenate(scaled, axis=0)
    return lax.dot_general(lower, scaled, (((0,), (0,)), ((), ())), precision=HIGHEST, preferred_element_type=F32)


def weights_of(pos, mine, other):
    e = pos[1]
    one = jnp.where(e == 0, mine, other)
    two = jnp.where(e == 0, other, mine)
    packed = jnp.concatenate([one[:32], two[:32]], axis=0)
    d, diagonal = one[32:33], one[33:34]
    turned = jnp.concatenate([packed, jnp.zeros((HALF, MEMBERS), F32)], axis=0).T
    row, lane = iota((HALF, MEMBERS), 0), iota((HALF, MEMBERS), 1)
    a = jnp.where(lane <= row, packed, turned[:HALF])
    c = pltpu.roll(jnp.where(lane > row, packed, turned[:HALF]), HALF, 1)
    c = jnp.where(lane == row + HALF, diagonal, c)
    top = jnp.where(lane < HALF, a, packed)
    bottom = jnp.where(lane < HALF, turned[HALF:], c)
    g = jnp.concatenate([top, bottom], axis=0)
    row, lane = iota((MEMBERS, MEMBERS), 0), iota((MEMBERS, MEMBERS), 1)
    x = g * (1.0 / MEMBERS) + jnp.where(row == lane, 1.0, 0.0)
    x = inverse(x)
    shift = jnp.sum(x * d, axis=1, keepdims=True) * (1.0 / MEMBERS)
    z = x + shift
    return z - jnp.mean(z, axis=0, keepdims=True) + 1.0 / MEMBERS


def second_run(pos, mine, other, fr, fo, table, weights, observed, k1, keep, send, FR, FO, H, U, V):
    k = weights_of(pos, mine[...], other[...])
    k1[...] = k
    for src, out in ((fr, FR), (fo, FO)):
        new = jnp.dot(src[...].reshape(EXT * WIDE, MEMBERS), k, precision=HIGHEST, preferred_element_type=F32)
        out[...] = new.reshape(EXT, WIDE, MEMBERS)
    forward(pos[0], table[...], FR, FO, H, U, V)
    gram(pos, H, weights[1], observed[1], keep, send)


def last_update(pos, mine, other, k1, own_p, other_p, out):
    k = jnp.dot(k1[...], weights_of(pos, mine[...], other[...]), precision=HIGHEST, preferred_element_type=F32)

    def emit(low, high, first):
        kt = k.T[first : first + HALF]
        for f in range(2):
            for r in range(ROWS):
                start = f * HALF * ROWS + r
                block = jnp.concatenate(
                    [low[pl.ds(start, HALF, stride=ROWS), :], high[pl.ds(start, HALF, stride=ROWS), :]],
                    axis=0,
                )
                out[pl.ds(start, HALF, stride=ROWS), :] = jnp.dot(
                    kt, block, precision=HIGHEST, preferred_element_type=F32
                )

    @pl.when(pos[1] == 0)
    def _():
        emit(own_p, other_p, 0)

    @pl.when(pos[1] == 1)
    def _():
        emit(other_p, own_p, HALF)


def swap(value):
    return lax.ppermute(value, "ens", [(0, 1), (1, 0)])


def moved(value, axes, by):
    n = lax.axis_size(axes)
    return lax.ppermute(value, axes, [(i, (i + by) % n) for i in range(n)])


def exchanged(value, axis, bits):
    n = lax.axis_size(axis)
    masks = [0]
    for bit in bits:
        masks += [m | bit for m in masks]
    terms = [value] + [lax.ppermute(value, axis, [(i, i ^ m) for i in range(n)]) for m in masks[1:]]
    while len(terms) > 1:
        terms = [a + b for a, b in zip(terms[::2], terms[1::2])]
    return terms[0]


def reduced(keep, send):
    value = keep + swap(send)
    for axis, bits in (("lat_0", (1, 2)), ("lat_1", (1, 2)), ("lon", (1,)), ("lon", (2, 4))):
        value = exchanged(value, axis, bits)
    return value, swap(value)


def call(kernel, out_shape, scalars, *args, scratch=()):
    return pl.pallas_call(
        kernel,
        out_shape=out_shape,
        in_specs=[SMEM] + [VMEM] * len(args),
        out_specs=jax.tree.map(lambda _: VMEM, out_shape),
        scratch_shapes=list(scratch),
        compiler_params=params(),
    )(scalars, *args)


def per_device(parameters, initial_height, initial_speed, obs_slots, obs_values, obs_precision):
    pos = jnp.stack([lax.axis_index(LAT), lax.axis_index("ens")]).astype(jnp.int32)
    own_p = parameters.reshape(2 * HALF * ROWS, COLS)
    other_p = swap(own_p)
    by_slot = [x[:, 0].transpose(0, 2, 1).reshape(16, 128) for x in (obs_slots, obs_values, obs_precision)]

    own, up2, dn2, obs = call(
        spread_members,
        [shape(OWN + INIT, 128), shape(216, 128), shape(216, 128), shape(128, 128)],
        pos, own_p, other_p, initial_height, initial_speed.reshape(16, COLS), by_slot[1], by_slot[2],
    )
    m2, p2 = moved(up2, LAT, 2), moved(dn2, LAT, -2)
    m1, p1 = moved(own, LAT, 1), moved(own, LAT, -1)

    obs = lax.all_to_all(obs, LAT_LON, 0, 0, tiled=True)
    weights, observed = call(scatter_obs, [shape(2, 512, 128), shape(2, 512, 128)], pos, by_slot[0], obs)

    right, left = pl.pallas_call(
        pack_edges,
        out_shape=[shape(EDGE, 128)] * 2,
        in_specs=[VMEM] * 6,
        out_specs=[VMEM] * 2,
        compiler_params=params(),
    )(own, m1, p1, m2, p2, weights)
    lz, rz = moved(right, LON_ENS, 1), moved(left, LON_ENS, -1)

    field = shape(EXT, WIDE, MEMBERS)
    half = shape(40, MEMBERS)
    square = shape(MEMBERS, MEMBERS)
    state = [pltpu.VMEM((EXT, WIDE, MEMBERS), F32)]
    ext_fr, ext_fo, table, keep, send = call(
        first_run, [field, field, square, half, half],
        pos, own, m1, p1, m2, p2, lz, rz, weights, observed,
        scratch=state * 3,
    )
    mine, other = reduced(keep, send)
    k1, keep, send = call(
        second_run, [square, half, half],
        pos, mine, other, ext_fr, ext_fo, table, weights, observed,
        scratch=state * 5,
    )
    mine, other = reduced(keep, send)
    out = call(last_update, shape(2 * HALF * ROWS, COLS), pos, mine, other, k1, own_p, other_p)
    return out.reshape(parameters.shape)


def solution(mesh):
    torus = Mesh(
        mesh.devices.reshape(4, 4, mesh.shape["lon"], mesh.shape["ens"]),
        ("lat_0", "lat_1", "lon", "ens"),
    )
    in_specs = (
        P(None, "ens", LAT, "lon"),
        P(LAT, "lon"),
        P(None, LAT, "lon"),
        P(None, LAT_LON, None, None),
        P(None, LAT_LON, None, None),
        P(None, LAT_LON, None, None),
    )
    out_specs = P(None, "ens", LAT, "lon")
    return jax.shard_map(
        per_device, mesh=torus, in_specs=in_specs, out_specs=out_specs, check_vma=False
    )
```

profile of v0, /device:TPU:1, one launch (start us, length us, event | category | flops | bytes accessed | tf_op | source)
XLA Modules:
  0.0 134.2 jit_solution(14229214610021968826)
XLA Ops:
  0.0 3.2 %collective-permute-start = (f32[1024,128]{1,0:T(8,128)}, f32[1024,128]{1,0:T(8,128)S(1)}, u32[]{:S(2)}, u32[]{:S(2)}) collective-permute-start(f32[1024,128]{1,0:T(8,128)} %bitcast.24), channel_id=1, source_target_pairs={{0,1},{1,0},{2,3},{3,2},{4,5},{5,4},{6,7},{7,6},{8,9},{9,8},{10,11... | collective-permute-start | bytes 1572872 | tf_op jit(solution)/shard_map/ppermute | solution.py:368
  3.3 1.7 %collective-permute-done.other.other_p = f32[1024,128]{1,0:T(8,128)S(1)} collective-permute-done((f32[1024,128]{1,0:T(8,128)}, f32[1024,128]{1,0:T(8,128)S(1)}, u32[]{:S(2)}, u32[]{:S(2)}) %collective-permute-start) | collective-permute-done | bytes 524320 | tf_op jit(solution)/shard_map/ppermute | solution.py:368
  10.4 3.2 %collective-permute-start.2 = (f32[1048,128]{1,0:T(8,128)S(1)}, f32[1048,128]{1,0:T(8,128)S(1)}, u32[]{:S(2)}, u32[]{:S(2)}) collective-permute-start(f32[1048,128]{1,0:T(8,128)S(1)} %get-tuple-element.21.own), channel_id=1, source_target_pairs={{0,240},{16,0},{32,16},{48,32},{64,48},{80,64},{96,80},{112,96},{1... | collective-permute-start | bytes 1609736 | tf_op jit(solution)/shard_map/ppermute | solution.py:373
  13.6 14.9 %all-to-all-start = ((f32[128,1,128]{2,1,0:T(1,128)}), f32[128,1,128]{2,1,0:T(1,128)S(1)}, u32[]{:S(2)}, u32[]{:S(2)}) async-start(f32[128,1,128]{2,1,0:T(1,128)} %bitcast.14), calls=%async_computation | async-start | bytes 131072 | tf_op jit(solution)/shard_map/all_to_all | solution.py:419
  28.5 2.2 %collective-permute-start.3 = (f32[216,128]{1,0:T(8,128)S(1)}, f32[216,128]{1,0:T(8,128)S(1)}, u32[]{:S(2)}, u32[]{:S(2)}) collective-permute-start(f32[216,128]{1,0:T(8,128)S(1)} %get-tuple-element.22), channel_id=1, source_target_pairs={{0,32},{16,48},{32,64},{48,80},{64,96},{80,112},{96,128},{112,144}... | collective-permute-start | bytes 331784 | tf_op jit(solution)/shard_map/ppermute | solution.py:373
  30.7 3.0 %collective-permute-start.4 = (f32[216,128]{1,0:T(8,128)S(1)}, f32[216,128]{1,0:T(8,128)S(1)}, u32[]{:S(2)}, u32[]{:S(2)}) collective-permute-start(f32[216,128]{1,0:T(8,128)S(1)} %get-tuple-element.23), channel_id=1, source_target_pairs={{0,224},{16,240},{32,0},{48,16},{64,32},{80,48},{96,64},{112,80},{... | collective-permute-start | bytes 331784 | tf_op jit(solution)/shard_map/ppermute | solution.py:373
  33.7 5.3 %all-to-all-done = f32[128,1,128]{2,1,0:T(1,128)S(1)} async-done(((f32[128,1,128]{2,1,0:T(1,128)}), f32[128,1,128]{2,1,0:T(1,128)S(1)}, u32[]{:S(2)}, u32[]{:S(2)}) %all-to-all-start) | async-done | bytes 65568 | tf_op jit(solution)/shard_map/all_to_all | solution.py:419
  41.3 2.5 %collective-permute-start.5 = (f32[696,128]{1,0:T(8,128)S(1)}, f32[696,128]{1,0:T(8,128)S(1)}, u32[]{:S(2)}, u32[]{:S(2)}) collective-permute-start(f32[696,128]{1,0:T(8,128)S(1)} %get-tuple-element.26), channel_id=1, source_target_pairs={{0,1},{1,2},{2,3},{3,4},{4,5},{5,6},{6,7},{7,8},{8,9},{9,10},{10,1... | collective-permute-start | bytes 1069064 | tf_op jit(solution)/shard_map/ppermute | solution.py:373
  43.8 4.3 %collective-permute-done.5.lz = f32[696,128]{1,0:T(8,128)S(1)} collective-permute-done((f32[696,128]{1,0:T(8,128)S(1)}, f32[696,128]{1,0:T(8,128)S(1)}, u32[]{:S(2)}, u32[]{:S(2)}) %collective-permute-start.5) | collective-permute-done | bytes 356384 | tf_op jit(solution)/shard_map/ppermute | solution.py:373
  48.1 2.8 %collective-permute-done.6.rz = f32[696,128]{1,0:T(8,128)S(1)} collective-permute-done((f32[696,128]{1,0:T(8,128)S(1)}, f32[696,128]{1,0:T(8,128)S(1)}, u32[]{:S(2)}, u32[]{:S(2)}) %collective-permute-start.6) | collective-permute-done | bytes 356384 | tf_op jit(solution)/shard_map/ppermute | solution.py:373
  50.9 5.5 %shard_map.67 = (f32[28,112,128]{2,1,0:T(8,128)S(1)}, f32[28,112,128]{2,1,0:T(8,128)S(1)}, f32[128,128]{1,0:T(8,128)S(1)}, f32[40,128]{1,0:T(8,128)S(1)}, f32[40,128]{1,0:T(8,128)S(1)}) custom-call(s32[2]{0:T(128)S(1)} %pad_add_fusion.pos, f32[1048,128]{1,0:T(8,128)S(1)} %get-tuple-element.21.own, f32[1048,128]{1,0:T(8,128)S(1)} %collective-permute-done.1.m1, ...), custom_call_target="tpu_custom_call" | custom-call | tf_op jit(solution)/shard_map/pallas_call | solution.py:395
  68.6 2.7 %collective-permute-done.14 = f32[40,128]{1,0:T(8,128)S(1)} collective-permute-done((f32[40,128]{1,0:T(8,128)S(1)}, f32[40,128]{1,0:T(8,128)S(1)}, u32[]{:S(2)}, u32[]{:S(2)}) %collective-permute-start.14) | collective-permute-done | bytes 20512 | tf_op jit(solution)/shard_map/ppermute | solution.py:381
  71.3 2.6 %collective-permute-start.17 = (f32[40,128]{1,0:T(8,128)S(1)}, f32[40,128]{1,0:T(8,128)S(1)}, u32[]{:S(2)}, u32[]{:S(2)}) collective-permute-start(f32[40,128]{1,0:T(8,128)S(1)} %add.77), channel_id=1, source_target_pairs={{0,12},{2,14},{4,8},{6,10},{8,4},{10,6},{12,0},{14,2},{1,13},{3,15... | collective-permute-start | bytes 61448 | tf_op jit(solution)/shard_map/ppermute | solution.py:381
  73.8 3.7 %collective-permute-start.16 = (f32[40,128]{1,0:T(8,128)S(1)}, f32[40,128]{1,0:T(8,128)S(1)}, u32[]{:S(2)}, u32[]{:S(2)}) collective-permute-start(f32[40,128]{1,0:T(8,128)S(1)} %add.77), channel_id=1, source_target_pairs={{0,8},{2,10},{4,12},{6,14},{8,0},{10,2},{12,4},{14,6},{1,9},{3,11}... | collective-permute-start | bytes 61448 | tf_op jit(solution)/shard_map/ppermute | solution.py:381
  77.6 2.8 %collective-permute-done.16 = f32[40,128]{1,0:T(8,128)S(1)} collective-permute-done((f32[40,128]{1,0:T(8,128)S(1)}, f32[40,128]{1,0:T(8,128)S(1)}, u32[]{:S(2)}, u32[]{:S(2)}) %collective-permute-start.16) | collective-permute-done | bytes 20512 | tf_op jit(solution)/shard_map/ppermute | solution.py:381
  81.2 5.6 %collective-permute-start.18 = (f32[40,128]{1,0:T(8,128)S(1)}, f32[40,128]{1,0:T(8,128)S(1)}, u32[]{:S(2)}, u32[]{:S(2)}) collective-permute-start(f32[40,128]{1,0:T(8,128)S(1)} %add_add_fusion.3.mine), channel_id=1, source_target_pairs={{0,1},{1,0},{2,3},{3,2},{4,5},{5,4},{6,7},{7,6},{8,9},{9,8},{10,11... | collective-permute-start | bytes 61448 | tf_op jit(solution)/shard_map/ppermute | solution.py:368
  87.7 10.8 %shard_map.68 = (f32[128,128]{1,0:T(8,128)S(1)}, f32[40,128]{1,0:T(8,128)S(1)}, f32[40,128]{1,0:T(8,128)S(1)}) custom-call(s32[2]{0:T(128)S(1)} %pad_add_fusion.pos, f32[40,128]{1,0:T(8,128)S(1)} %add_add_fusion.3.mine, f32[40,128]{1,0:T(8,128)S(1)} %collective-permute-done.18.other, f32[28,112,128]{2,1,0:T(8,128)S(1)} %get-tuple-element.31.fr, ...), custom_call_target="tpu_custom_call" | custom-call | tf_op jit(solution)/shard_map/pallas_call | solution.py:395
  109.0 1.6 %collective-permute-done.24 = f32[40,128]{1,0:T(8,128)S(1)} collective-permute-done((f32[40,128]{1,0:T(8,128)S(1)}, f32[40,128]{1,0:T(8,128)S(1)}, u32[]{:S(2)}, u32[]{:S(2)}) %collective-permute-start.24) | collective-permute-done | bytes 20512 | tf_op jit(solution)/shard_map/ppermute | solution.py:381
  110.6 1.8 %collective-permute-start.26 = (f32[40,128]{1,0:T(8,128)S(1)}, f32[40,128]{1,0:T(8,128)S(1)}, u32[]{:S(2)}, u32[]{:S(2)}) collective-permute-start(f32[40,128]{1,0:T(8,128)S(1)} %add_add_fusion.1), channel_id=1, source_target_pairs={{0,2},{2,0},{4,6},{6,4},{8,10},{10,8},{12,14},{14,12},{1,3},{3,1},... | collective-permute-start | bytes 61448 | tf_op jit(solution)/shard_map/ppermute | solution.py:381
  114.8 2.6 %collective-permute-start.28 = (f32[40,128]{1,0:T(8,128)S(1)}, f32[40,128]{1,0:T(8,128)S(1)}, u32[]{:S(2)}, u32[]{:S(2)}) collective-permute-start(f32[40,128]{1,0:T(8,128)S(1)} %add.88), channel_id=1, source_target_pairs={{0,8},{2,10},{4,12},{6,14},{8,0},{10,2},{12,4},{14,6},{1,9},{3,11}... | collective-permute-start | bytes 61448 | tf_op jit(solution)/shard_map/ppermute | solution.py:381
  117.5 1.8 %collective-permute-start.27 = (f32[40,128]{1,0:T(8,128)S(1)}, f32[40,128]{1,0:T(8,128)S(1)}, u32[]{:S(2)}, u32[]{:S(2)}) collective-permute-start(f32[40,128]{1,0:T(8,128)S(1)} %add.88), channel_id=1, source_target_pairs={{0,4},{2,6},{4,0},{6,2},{8,12},{10,14},{12,8},{14,10},{1,5},{3,7},... | collective-permute-start | bytes 61448 | tf_op jit(solution)/shard_map/ppermute | solution.py:381
  119.3 2.1 %collective-permute-done.28 = f32[40,128]{1,0:T(8,128)S(1)} collective-permute-done((f32[40,128]{1,0:T(8,128)S(1)}, f32[40,128]{1,0:T(8,128)S(1)}, u32[]{:S(2)}, u32[]{:S(2)}) %collective-permute-start.28) | collective-permute-done | bytes 20512 | tf_op jit(solution)/shard_map/ppermute | solution.py:381
  121.4 5.8 %collective-permute-start.30 = (f32[40,128]{1,0:T(8,128)S(1)}, f32[40,128]{1,0:T(8,128)S(1)}, u32[]{:S(2)}, u32[]{:S(2)}) collective-permute-start(f32[40,128]{1,0:T(8,128)S(1)} %add_add_fusion.mine), channel_id=1, source_target_pairs={{0,1},{1,0},{2,3},{3,2},{4,5},{5,4},{6,7},{7,6},{8,9},{9,8},{10,11... | collective-permute-start | bytes 61448 | tf_op jit(solution)/shard_map/ppermute | solution.py:368
  128.0 6.2 %shard_map.69 = f32[1024,128]{1,0:T(8,128)} custom-call(s32[2]{0:T(128)S(1)} %pad_add_fusion.pos, f32[40,128]{1,0:T(8,128)S(1)} %add_add_fusion.mine, f32[40,128]{1,0:T(8,128)S(1)} %collective-permute-done.30.other, f32[128,128]{1,0:T(8,128)S(1)} %get-tuple-element.36.k1, f32[1024,128]{1,0:T(8,128)S(1)} %bitcast.26, ...), custom_call_target="tpu_custom_call" | custom-call | tf_op jit(solution)/shard_map/pallas_call | solution.py:395
  (71 shorter events, 35.4 us)
Async XLA Ops:
  0.0 5.0 %collective-permute-start = (f32[1024,128]{1,0:T(8,128)}, f32[1024,128]{1,0:T(8,128)S(1)}, u32[]{:S(2)}, u32[]{:S(2)}) collective-permute-start(f32[1024,128]{1,0:T(8,128)} %bitcast.24), channel_id=1, source_target_pairs={{0,1},{1,0},{2,3},{3,2},{4,5},{5,4},{6,7},{7,6},{8,9},{9,8},{10,11... | collective-permute-start | bytes 1572872 | tf_op jit(solution)/shard_map/ppermute | solution.py:368
  10.4 30.8 %collective-permute-start.2 = (f32[1048,128]{1,0:T(8,128)S(1)}, f32[1048,128]{1,0:T(8,128)S(1)}, u32[]{:S(2)}, u32[]{:S(2)}) collective-permute-start(f32[1048,128]{1,0:T(8,128)S(1)} %get-tuple-element.21.own), channel_id=1, source_target_pairs={{0,240},{16,0},{32,16},{48,32},{64,48},{80,64},{96,80},{112,96},{1... | collective-permute-start | bytes 1609736 | tf_op jit(solution)/shard_map/ppermute | solution.py:373
  13.6 27.6 %collective-permute-start.1 = (f32[1048,128]{1,0:T(8,128)S(1)}, f32[1048,128]{1,0:T(8,128)S(1)}, u32[]{:S(2)}, u32[]{:S(2)}) collective-permute-start(f32[1048,128]{1,0:T(8,128)S(1)} %get-tuple-element.21.own), channel_id=1, source_target_pairs={{0,16},{16,32},{32,48},{48,64},{64,80},{80,96},{96,112},{112,128},... | collective-permute-start | bytes 1609736 | tf_op jit(solution)/shard_map/ppermute | solution.py:373
  13.6 25.4 %all-to-all-start = ((f32[128,1,128]{2,1,0:T(1,128)}), f32[128,1,128]{2,1,0:T(1,128)S(1)}, u32[]{:S(2)}, u32[]{:S(2)}) async-start(f32[128,1,128]{2,1,0:T(1,128)} %bitcast.14), calls=%async_computation | async-start | bytes 131072 | tf_op jit(solution)/shard_map/all_to_all | solution.py:419
  28.5 12.6 %collective-permute-start.3 = (f32[216,128]{1,0:T(8,128)S(1)}, f32[216,128]{1,0:T(8,128)S(1)}, u32[]{:S(2)}, u32[]{:S(2)}) collective-permute-start(f32[216,128]{1,0:T(8,128)S(1)} %get-tuple-element.22), channel_id=1, source_target_pairs={{0,32},{16,48},{32,64},{48,80},{64,96},{80,112},{96,128},{112,144}... | collective-permute-start | bytes 331784 | tf_op jit(solution)/shard_map/ppermute | solution.py:373
  30.7 10.5 %collective-permute-start.4 = (f32[216,128]{1,0:T(8,128)S(1)}, f32[216,128]{1,0:T(8,128)S(1)}, u32[]{:S(2)}, u32[]{:S(2)}) collective-permute-start(f32[216,128]{1,0:T(8,128)S(1)} %get-tuple-element.23), channel_id=1, source_target_pairs={{0,224},{16,240},{32,0},{48,16},{64,32},{80,48},{96,64},{112,80},{... | collective-permute-start | bytes 331784 | tf_op jit(solution)/shard_map/ppermute | solution.py:373
  41.3 6.8 %collective-permute-start.5 = (f32[696,128]{1,0:T(8,128)S(1)}, f32[696,128]{1,0:T(8,128)S(1)}, u32[]{:S(2)}, u32[]{:S(2)}) collective-permute-start(f32[696,128]{1,0:T(8,128)S(1)} %get-tuple-element.26), channel_id=1, source_target_pairs={{0,1},{1,2},{2,3},{3,4},{4,5},{5,6},{6,7},{7,8},{8,9},{9,10},{10,1... | collective-permute-start | bytes 1069064 | tf_op jit(solution)/shard_map/ppermute | solution.py:373
  43.8 7.1 %collective-permute-start.6 = (f32[696,128]{1,0:T(8,128)S(1)}, f32[696,128]{1,0:T(8,128)S(1)}, u32[]{:S(2)}, u32[]{:S(2)}) collective-permute-start(f32[696,128]{1,0:T(8,128)S(1)} %get-tuple-element.27), channel_id=1, source_target_pairs={{0,15},{1,0},{2,1},{3,2},{4,3},{5,4},{6,5},{7,6},{8,7},{9,8},{10,9... | collective-permute-start | bytes 1069064 | tf_op jit(solution)/shard_map/ppermute | solution.py:373
  58.0 3.8 %collective-permute-start.10 = (f32[40,128]{1,0:T(8,128)S(1)}, f32[40,128]{1,0:T(8,128)S(1)}, u32[]{:S(2)}, u32[]{:S(2)}) collective-permute-start(f32[40,128]{1,0:T(8,128)S(1)} %add.70), channel_id=1, source_target_pairs={{0,192},{64,128},{128,64},{192,0},{1,193},{65,129},{129,65},{193,1... | collective-permute-start | bytes 61448 | tf_op jit(solution)/shard_map/ppermute | solution.py:381
  58.4 4.1 %collective-permute-start.9 = (f32[40,128]{1,0:T(8,128)S(1)}, f32[40,128]{1,0:T(8,128)S(1)}, u32[]{:S(2)}, u32[]{:S(2)}) collective-permute-start(f32[40,128]{1,0:T(8,128)S(1)} %add.70), channel_id=1, source_target_pairs={{0,128},{64,192},{128,0},{192,64},{1,129},{65,193},{129,1},{193,65... | collective-permute-start | bytes 61448 | tf_op jit(solution)/shard_map/ppermute | solution.py:381
  63.0 4.1 %collective-permute-start.13 = (f32[40,128]{1,0:T(8,128)S(1)}, f32[40,128]{1,0:T(8,128)S(1)}, u32[]{:S(2)}, u32[]{:S(2)}) collective-permute-start(f32[40,128]{1,0:T(8,128)S(1)} %add_add_fusion.5), channel_id=1, source_target_pairs={{0,48},{16,32},{32,16},{48,0},{1,49},{17,33},{33,17},{49,1},{2,50}... | collective-permute-start | bytes 61448 | tf_op jit(solution)/shard_map/ppermute | solution.py:381
  64.3 4.1 %collective-permute-start.12 = (f32[40,128]{1,0:T(8,128)S(1)}, f32[40,128]{1,0:T(8,128)S(1)}, u32[]{:S(2)}, u32[]{:S(2)}) collective-permute-start(f32[40,128]{1,0:T(8,128)S(1)} %add_add_fusion.5), channel_id=1, source_target_pairs={{0,32},{16,48},{32,0},{48,16},{1,33},{17,49},{33,1},{49,17},{2,34}... | collective-permute-start | bytes 61448 | tf_op jit(solution)/shard_map/ppermute | solution.py:381
  71.3 6.3 %collective-permute-start.17 = (f32[40,128]{1,0:T(8,128)S(1)}, f32[40,128]{1,0:T(8,128)S(1)}, u32[]{:S(2)}, u32[]{:S(2)}) collective-permute-start(f32[40,128]{1,0:T(8,128)S(1)} %add.77), channel_id=1, source_target_pairs={{0,12},{2,14},{4,8},{6,10},{8,4},{10,6},{12,0},{14,2},{1,13},{3,15... | collective-permute-start | bytes 61448 | tf_op jit(solution)/shard_map/ppermute | solution.py:381
  73.8 6.5 %collective-permute-start.16 = (f32[40,128]{1,0:T(8,128)S(1)}, f32[40,128]{1,0:T(8,128)S(1)}, u32[]{:S(2)}, u32[]{:S(2)}) collective-permute-start(f32[40,128]{1,0:T(8,128)S(1)} %add.77), channel_id=1, source_target_pairs={{0,8},{2,10},{4,12},{6,14},{8,0},{10,2},{12,4},{14,6},{1,9},{3,11}... | collective-permute-start | bytes 61448 | tf_op jit(solution)/shard_map/ppermute | solution.py:381
  77.6 3.6 %collective-permute-start.15 = (f32[40,128]{1,0:T(8,128)S(1)}, f32[40,128]{1,0:T(8,128)S(1)}, u32[]{:S(2)}, u32[]{:S(2)}) collective-permute-start(f32[40,128]{1,0:T(8,128)S(1)} %add.77), channel_id=1, source_target_pairs={{0,4},{2,6},{4,0},{6,2},{8,12},{10,14},{12,8},{14,10},{1,5},{3,7},... | collective-permute-start | bytes 61448 | tf_op jit(solution)/shard_map/ppermute | solution.py:381
  81.2 6.4 %collective-permute-start.18 = (f32[40,128]{1,0:T(8,128)S(1)}, f32[40,128]{1,0:T(8,128)S(1)}, u32[]{:S(2)}, u32[]{:S(2)}) collective-permute-start(f32[40,128]{1,0:T(8,128)S(1)} %add_add_fusion.3.mine), channel_id=1, source_target_pairs={{0,1},{1,0},{2,3},{3,2},{4,5},{5,4},{6,7},{7,6},{8,9},{9,8},{10,11... | collective-permute-start | bytes 61448 | tf_op jit(solution)/shard_map/ppermute | solution.py:368
  99.8 3.8 %collective-permute-start.22 = (f32[40,128]{1,0:T(8,128)S(1)}, f32[40,128]{1,0:T(8,128)S(1)}, u32[]{:S(2)}, u32[]{:S(2)}) collective-permute-start(f32[40,128]{1,0:T(8,128)S(1)} %add.81), channel_id=1, source_target_pairs={{0,192},{64,128},{128,64},{192,0},{1,193},{65,129},{129,65},{193,1... | collective-permute-start | bytes 61448 | tf_op jit(solution)/shard_map/ppermute | solution.py:381
  100.9 4.1 %collective-permute-start.21 = (f32[40,128]{1,0:T(8,128)S(1)}, f32[40,128]{1,0:T(8,128)S(1)}, u32[]{:S(2)}, u32[]{:S(2)}) collective-permute-start(f32[40,128]{1,0:T(8,128)S(1)} %add.81), channel_id=1, source_target_pairs={{0,128},{64,192},{128,0},{192,64},{1,129},{65,193},{129,1},{193,65... | collective-permute-start | bytes 61448 | tf_op jit(solution)/shard_map/ppermute | solution.py:381
  105.1 3.9 %collective-permute-start.25 = (f32[40,128]{1,0:T(8,128)S(1)}, f32[40,128]{1,0:T(8,128)S(1)}, u32[]{:S(2)}, u32[]{:S(2)}) collective-permute-start(f32[40,128]{1,0:T(8,128)S(1)} %add_add_fusion.2), channel_id=1, source_target_pairs={{0,48},{16,32},{32,16},{48,0},{1,49},{17,33},{33,17},{49,1},{2,50}... | collective-permute-start | bytes 61448 | tf_op jit(solution)/shard_map/ppermute | solution.py:381
  106.5 4.1 %collective-permute-start.24 = (f32[40,128]{1,0:T(8,128)S(1)}, f32[40,128]{1,0:T(8,128)S(1)}, u32[]{:S(2)}, u32[]{:S(2)}) collective-permute-start(f32[40,128]{1,0:T(8,128)S(1)} %add_add_fusion.2), channel_id=1, source_target_pairs={{0,32},{16,48},{32,0},{48,16},{1,33},{17,49},{33,1},{49,17},{2,34}... | collective-permute-start | bytes 61448 | tf_op jit(solution)/shard_map/ppermute | solution.py:381
  113.6 5.7 %collective-permute-start.29 = (f32[40,128]{1,0:T(8,128)S(1)}, f32[40,128]{1,0:T(8,128)S(1)}, u32[]{:S(2)}, u32[]{:S(2)}) collective-permute-start(f32[40,128]{1,0:T(8,128)S(1)} %add.88), channel_id=1, source_target_pairs={{0,12},{2,14},{4,8},{6,10},{8,4},{10,6},{12,0},{14,2},{1,13},{3,15... | collective-permute-start | bytes 61448 | tf_op jit(solution)/shard_map/ppermute | solution.py:381
  114.8 6.5 %collective-permute-start.28 = (f32[40,128]{1,0:T(8,128)S(1)}, f32[40,128]{1,0:T(8,128)S(1)}, u32[]{:S(2)}, u32[]{:S(2)}) collective-permute-start(f32[40,128]{1,0:T(8,128)S(1)} %add.88), channel_id=1, source_target_pairs={{0,8},{2,10},{4,12},{6,14},{8,0},{10,2},{12,4},{14,6},{1,9},{3,11}... | collective-permute-start | bytes 61448 | tf_op jit(solution)/shard_map/ppermute | solution.py:381
  117.5 3.9 %collective-permute-start.27 = (f32[40,128]{1,0:T(8,128)S(1)}, f32[40,128]{1,0:T(8,128)S(1)}, u32[]{:S(2)}, u32[]{:S(2)}) collective-permute-start(f32[40,128]{1,0:T(8,128)S(1)} %add.88), channel_id=1, source_target_pairs={{0,4},{2,6},{4,0},{6,2},{8,12},{10,14},{12,8},{14,10},{1,5},{3,7},... | collective-permute-start | bytes 61448 | tf_op jit(solution)/shard_map/ppermute | solution.py:381
  121.4 6.6 %collective-permute-start.30 = (f32[40,128]{1,0:T(8,128)S(1)}, f32[40,128]{1,0:T(8,128)S(1)}, u32[]{:S(2)}, u32[]{:S(2)}) collective-permute-start(f32[40,128]{1,0:T(8,128)S(1)} %add_add_fusion.mine), channel_id=1, source_target_pairs={{0,1},{1,0},{2,3},{3,2},{4,5},{5,4},{6,7},{7,6},{8,9},{9,8},{10,11... | collective-permute-start | bytes 61448 | tf_op jit(solution)/shard_map/ppermute | solution.py:368
  (15 other events, 66.2 us)
where the time goes:
time: 135 us; the launch traced here: 134 us
  starting transfers between devices  68.9 us (51%)
  waiting for transfers between devices  34.9 us (26%)
  Pallas kernels  25.6 us (19%)
  local copies, waits for them, and re-layouts  4.52 us (3%)
    ppermute x20, starting transfers between devices, exchanged(): lax.ppermute(value, axis, [(i, i ^ m) for i in range(n)])  27.3 us
    pallas_call x5, Pallas kernels, call(): pl.pallas_call(kernel, out_shape=out_shape, in_specs=[SMEM] + [VMEM] * le...  25.6 us
    ppermute x20, waiting for transfers between devices, exchanged(): lax.ppermute(value, axis, [(i, i ^ m) for i in range(n)])  17.4 us
    ppermute x5, starting transfers between devices, swap(): return lax.ppermute(value, 'ens', [(0, 1), (1, 0)])  15.9 us
    all_to_all x1, starting transfers between devices, per_device(): obs = lax.all_to_all(obs, LAT_LON, 0, 0, tiled=True)  14.9 us
    ppermute x6, starting transfers between devices, moved(): return lax.ppermute(value, axes, [(i, (i + by) % n) for i in range(n)])  10.9 us
    ppermute x6, waiting for transfers between devices, moved(): return lax.ppermute(value, axes, [(i, (i + by) % n) for i in range(n)])  7.11 us
    all_to_all x1, waiting for transfers between devices, per_device(): obs = lax.all_to_all(obs, LAT_LON, 0, 0, tiled=True)  5.33 us
  transfers between devices with their start and end apart: 32, of which 22 were waited for; matrix products, arithmetic and copies ran while one was open for 0% of the time, Pallas kernels for 1%

commit v1 on v0

--- a/solution.py
+++ b/solution.py
@@ -48,7 +48,20 @@
     return lax.broadcasted_iota(jnp.int32, dims, axis)
 
 
-def spread_members(pos, own, other, height, speed, values, precision, out, up2, dn2, obs):
+def gather_small(height, speed, values, precision, own, fields, obs):
+    del own
+    fields[:ROWS] = height[...]
+    fields[ROWS:] = speed[...]
+    lines = [values[...], precision[...], jnp.zeros((96, MEMBERS), F32)]
+    by_owner = jnp.concatenate(lines, axis=0).T
+    for x in range(4):
+        parts = [by_owner[(4 * x + y) * 8 : (4 * x + y + 1) * 8] for y in range(4)]
+        obs[8 * x : 8 * x + 8] = (
+            parts[0] + pltpu.roll(parts[1], 32, 1) + pltpu.roll(parts[2], 64, 1) + pltpu.roll(parts[3], 96, 1)
+        )
+
+
+def spread_members(pos, own, other, fields, out, up2, dn2):
     def emit(low, high, first):
         for f in range(2):
             for r in range(ROWS):
@@ -70,10 +83,7 @@
                     dn2[2 * HALF : 3 * HALF] = turned
 
     for ref, at in ((out, OWN), (up2, 3 * HALF), (dn2, 3 * HALF)):
-        ref[at : at + ROWS] = height[...]
-        ref[at + ROWS : at + INIT] = speed[...]
-    lines = [values[...], precision[...], jnp.zeros((96, MEMBERS), F32)]
-    obs[...] = jnp.concatenate(lines, axis=0).T
+        ref[at : at + INIT] = fields[...]
 
     @pl.when(pos[1] == 0)
     def _():
@@ -95,8 +105,7 @@
 
 
 EDGE_ROWS = edge_rows()
-EDGE_FIELDS = sum(n for _, _, n in EDGE_ROWS)
-EDGE = EDGE_FIELDS + 5 * INIT
+EDGE = sum(n for _, _, n in EDGE_ROWS)
 
 
 def row_source(field, r, own, m1, p1, m2, p2):
@@ -117,7 +126,8 @@
     return ((m2, 3 * HALF), (m1, OWN), (own, OWN), (p1, OWN), (p2, 3 * HALF))
 
 
-def pack_edges(own, m1, p1, m2, p2, _, right, left):
+def pack_edges(own, m1, p1, m2, p2, obs, right, left):
+    del obs
     at = 0
     for field, r, n in EDGE_ROWS:
         ref, start = row_source(field, r, own, m1, p1, m2, p2)
@@ -131,8 +141,15 @@
         at += INIT
 
 
-def scatter_obs(pos, slots, received, weights, observed):
-    received = received[...].T
+def scatter_obs(pos, slots, part0, part1, part2, part3, weights, observed):
+    y = pos[2]
+    parts = [pltpu.roll(part[...], (4 - y) * 32 % COLS, 1) for part in (part0, part1, part2, part3)]
+    by_y = []
+    for k in range(4):
+        m = y ^ k
+        by_y.append(jnp.where(m < 2, jnp.where(m == 0, parts[0], parts[1]), jnp.where(m == 2, parts[2], parts[3])))
+    tiles = [by_y[k][8 * x : 8 * x + 8] for x in range(4) for k in range(4)]
+    received = jnp.concatenate(tiles, axis=0).T
     values, precision = received[:16], received[16:32]
     lines = ROWS * HALF
     k = iota((lines, MEMBERS), 0)
@@ -155,7 +172,6 @@
 
 
 def initial_table(pos, tiles, lz, rz):
-    first = EDGE_FIELDS
     lane = iota((ROWS, COLS), 1)
     row = iota((ROWS, COLS), 0)
     e = pos[1]
@@ -163,7 +179,7 @@
     for k, (ref, start) in enumerate(tiles):
         for f in range(3):
             own = ref[start + f * ROWS : start + (f + 1) * ROWS]
-            at = first + k * INIT + f * ROWS
+            at = EDGE + k * INIT + f * ROWS
             before = lz[at : at + ROWS]
             after = rz[at : at + ROWS]
             low = pltpu.roll(jnp.where(lane >= 112, before, own), 16, 1)
@@ -234,7 +250,7 @@
             sweep(speed_row, reach - 1, a, b)
 
 
-def gram(pos, H, weights, observed, keep, send):
+def gram(H, weights, observed, total):
     lines = ROWS * HALF
     h = H[10:18, LEFT:RIGHT].reshape(lines, MEMBERS)
     centre = jnp.mean(h, axis=1, keepdims=True)
@@ -248,14 +264,10 @@
     diagonal = jnp.sum(jnp.where(lane == row + HALF, bottom, 0.0), axis=0, keepdims=True)
     line = iota((8, MEMBERS), 0)
     rest = jnp.where(line == 0, d, jnp.where(line == 1, diagonal, 0.0))
-    one = jnp.concatenate([packed[:32], rest], axis=0)
-    two = jnp.concatenate([packed[32:], jnp.zeros((8, MEMBERS), F32)], axis=0)
-    e = pos[1]
-    keep[...] = jnp.where(e == 0, one, two)
-    send[...] = jnp.where(e == 0, two, one)
-
-
-def first_run(pos, own, m1, p1, m2, p2, lz, rz, weights, observed, FR, FO, table, keep, send, H, U, V):
+    total[...] = jnp.concatenate([packed, rest], axis=0)
+
+
+def first_run(pos, own, m1, p1, m2, p2, lz, rz, weights, observed, FR, FO, table, total, H, U, V):
     at = 0
     for field, r, n in EDGE_ROWS:
         ref, begin = row_source(field, r, own, m1, p1, m2, p2)
@@ -270,7 +282,7 @@
         out[r, RIGHT : RIGHT + n] = east
     table[...] = initial_table(pos, initial_tiles(own, m1, p1, m2, p2), lz, rz)
     forward(pos[0], table[...], FR, FO, H, U, V)
-    gram(pos, H, weights[0], observed[0], keep, send)
+    gram(H, weights[0], observed[0], total)
 
 
 def inverse(x):
@@ -308,11 +320,8 @@
 
 
 def weights_of(pos, mine, other):
-    e = pos[1]
-    one = jnp.where(e == 0, mine, other)
-    two = jnp.where(e == 0, other, mine)
-    packed = jnp.concatenate([one[:32], two[:32]], axis=0)
-    d, diagonal = one[32:33], one[33:34]
+    total = jnp.where(pos[1] == 1, mine, other)
+    packed, d, diagonal = total[:HALF], total[HALF : HALF + 1], total[HALF + 1 : HALF + 2]
     turned = jnp.concatenate([packed, jnp.zeros((HALF, MEMBERS), F32)], axis=0).T
     row, lane = iota((HALF, MEMBERS), 0), iota((HALF, MEMBERS), 1)
     a = jnp.where(lane <= row, packed, turned[:HALF])
@@ -329,14 +338,14 @@
     return z - jnp.mean(z, axis=0, keepdims=True) + 1.0 / MEMBERS
 
 
-def second_run(pos, mine, other, fr, fo, table, weights, observed, k1, keep, send, FR, FO, H, U, V):
+def second_run(pos, mine, other, fr, fo, table, weights, observed, k1, total, FR, FO, H, U, V):
     k = weights_of(pos, mine[...], other[...])
     k1[...] = k
     for src, out in ((fr, FR), (fo, FO)):
         new = jnp.dot(src[...].reshape(EXT * WIDE, MEMBERS), k, precision=HIGHEST, preferred_element_type=F32)
         out[...] = new.reshape(EXT, WIDE, MEMBERS)
     forward(pos[0], table[...], FR, FO, H, U, V)
-    gram(pos, H, weights[1], observed[1], keep, send)
+    gram(H, weights[1], observed[1], total)
 
 
 def last_update(pos, mine, other, k1, own_p, other_p, out):
@@ -374,76 +383,77 @@
 
 
 def exchanged(value, axis, bits):
-    n = lax.axis_size(axis)
     masks = [0]
     for bit in bits:
         masks += [m | bit for m in masks]
-    terms = [value] + [lax.ppermute(value, axis, [(i, i ^ m) for i in range(n)]) for m in masks[1:]]
+    terms = [value]
+    for m in masks[1:]:
+        pairs = [(2 * i + 1, 2 * (i ^ m) + 1) for i in range(lax.axis_size(axis))]
+        terms.append(lax.ppermute(value, (axis, "ens"), pairs))
     while len(terms) > 1:
         terms = [a + b for a, b in zip(terms[::2], terms[1::2])]
     return terms[0]
 
 
-def reduced(keep, send):
-    value = keep + swap(send)
+def reduced(total):
+    value = total + lax.ppermute(total, "ens", [(0, 1)])
     for axis, bits in (("lat_0", (1, 2)), ("lat_1", (1, 2)), ("lon", (1,)), ("lon", (2, 4))):
         value = exchanged(value, axis, bits)
-    return value, swap(value)
+    return value, lax.ppermute(value, "ens", [(1, 0)])
 
 
 def call(kernel, out_shape, scalars, *args, scratch=()):
+    scalars = [] if scalars is None else [scalars]
     return pl.pallas_call(
         kernel,
         out_shape=out_shape,
-        in_specs=[SMEM] + [VMEM] * len(args),
+        in_specs=[SMEM] * len(scalars) + [VMEM] * len(args),
         out_specs=jax.tree.map(lambda _: VMEM, out_shape),
         scratch_shapes=list(scratch),
         compiler_params=params(),
-    )(scalars, *args)
+    )(*scalars, *args)
 
 
 def per_device(parameters, initial_height, initial_speed, obs_slots, obs_values, obs_precision):
-    pos = jnp.stack([lax.axis_index(LAT), lax.axis_index("ens")]).astype(jnp.int32)
+    pos = jnp.stack([lax.axis_index(a) for a in (LAT, "ens", "lat_1")]).astype(jnp.int32)
     own_p = parameters.reshape(2 * HALF * ROWS, COLS)
     other_p = swap(own_p)
     by_slot = [x[:, 0].transpose(0, 2, 1).reshape(16, 128) for x in (obs_slots, obs_values, obs_precision)]
 
-    own, up2, dn2, obs = call(
-        spread_members,
-        [shape(OWN + INIT, 128), shape(216, 128), shape(216, 128), shape(128, 128)],
-        pos, own_p, other_p, initial_height, initial_speed.reshape(16, COLS), by_slot[1], by_slot[2],
+    fields, obs = call(
+        gather_small, [shape(INIT, 128), shape(32, 128)],
+        None, initial_height, initial_speed.reshape(16, COLS), by_slot[1], by_slot[2], own_p,
+    )
+    own, up2, dn2 = call(
+        spread_members, [shape(OWN + INIT, 128), shape(216, 128), shape(216, 128)], pos, own_p, other_p, fields
     )
     m2, p2 = moved(up2, LAT, 2), moved(dn2, LAT, -2)
     m1, p1 = moved(own, LAT, 1), moved(own, LAT, -1)
 
-    obs = lax.all_to_all(obs, LAT_LON, 0, 0, tiled=True)
-    weights, observed = call(scatter_obs, [shape(2, 512, 128), shape(2, 512, 128)], pos, by_slot[0], obs)
-
-    right, left = pl.pallas_call(
-        pack_edges,
-        out_shape=[shape(EDGE, 128)] * 2,
-        in_specs=[VMEM] * 6,
-        out_specs=[VMEM] * 2,
-        compiler_params=params(),
-    )(own, m1, p1, m2, p2, weights)
+    obs = lax.all_to_all(obs, ("lat_0", "lon"), 0, 0, tiled=True)
+    parts = [obs] + [lax.ppermute(obs, "lat_1", [(i, i ^ m) for i in range(4)]) for m in (1, 2, 3)]
+    weights, observed = call(scatter_obs, [shape(2, 512, 128), shape(2, 512, 128)], pos, by_slot[0], *parts)
+
+    edge = shape(EDGE + 5 * INIT, 128)
+    right, left = call(pack_edges, [edge, edge], None, own, m1, p1, m2, p2, obs)
     lz, rz = moved(right, LON_ENS, 1), moved(left, LON_ENS, -1)
 
     field = shape(EXT, WIDE, MEMBERS)
-    half = shape(40, MEMBERS)
+    sums = shape(HALF + 8, MEMBERS)
     square = shape(MEMBERS, MEMBERS)
     state = [pltpu.VMEM((EXT, WIDE, MEMBERS), F32)]
-    ext_fr, ext_fo, table, keep, send = call(
-        first_run, [field, field, square, half, half],
+    ext_fr, ext_fo, table, total = call(
+        first_run, [field, field, square, sums],
         pos, own, m1, p1, m2, p2, lz, rz, weights, observed,
         scratch=state * 3,
     )
-    mine, other = reduced(keep, send)
-    k1, keep, send = call(
-        second_run, [square, half, half],
+    mine, other = reduced(total)
+    k1, total = call(
+        second_run, [square, sums],
         pos, mine, other, ext_fr, ext_fo, table, weights, observed,
         scratch=state * 5,
     )
-    mine, other = reduced(keep, send)
+    mine, other = reduced(total)
     out = call(last_update, shape(2 * HALF * ROWS, COLS), pos, mine, other, k1, own_p, other_p)
     return out.reshape(parameters.shape)
 

time: 135 us -> 166 us (1.23)
  starting transfers between devices: 68.9 us -> 86.7 us
  blocking collectives: 0 us -> 17 us
  waiting for transfers between devices: 34.9 us -> 30.6 us
    ppermute x20 -> x27, starting transfers between devices: 27.3 us -> 72.7 us  [the longest x20 63.4 us: exchanged(): terms.append(lax.ppermute(value, (axis, 'ens'), pairs))]
    all_to_all x0 -> x1, blocking collectives: none -> 17 us  [per_device(): obs = lax.all_to_all(obs, ('lat_0', 'lon'), 0, 0, tiled=True)]
    all_to_all x1 -> x0, starting transfers between devices: 14.9 us -> none  [per_device(): obs = lax.all_to_all(obs, LAT_LON, 0, 0, tiled=True)]
    ppermute x20 -> x27, waiting for transfers between devices: 17.4 us -> 30.6 us  [the longest x20 19 us: exchanged(): terms.append(lax.ppermute(value, (axis, 'ens'), pairs))]
    ppermute x5 -> x1, starting transfers between devices: 15.9 us -> 3.24 us  [swap(): return lax.ppermute(value, 'ens', [(0, 1), (1, 0)])]
    ppermute x6, waiting for transfers between devices: 7.11 us -> 0.02 us  [moved(): return lax.ppermute(value, axes, [(i, (i + by) % n) for i in range(n)])]
    all_to_all x1 -> x0, waiting for transfers between devices: 5.33 us -> none  [per_device(): obs = lax.all_to_all(obs, LAT_LON, 0, 0, tiled=True)]
    ppermute x5 -> x1, waiting for transfers between devices: 5.05 us -> 0.01 us  [swap(): return lax.ppermute(value, 'ens', [(0, 1), (1, 0)])]
  transfers between devices with their start and end apart: 32 -> 34, of which waited for: 22 -> 16; matrix products, arithmetic and copies ran while one was open for 0% -> 0% of each run, Pallas kernels for 1% -> 1%
where the time goes in v1:
time: 166 us; the launch traced here: 165 us
  starting transfers between devices  86.7 us (52%)
  waiting for transfers between devices  30.6 us (18%)
  Pallas kernels  25 us (15%)
  blocking collectives  17 us (10%)
  local copies, waits for them, and re-layouts  4.87 us (3%)
    ppermute x20, starting transfers between devices, exchanged(): terms.append(lax.ppermute(value, (axis, 'ens'), pairs))  63.4 us
    pallas_call x7, Pallas kernels, call(): pl.pallas_call(kernel, out_shape=out_shape, in_specs=[SMEM] * len(scalars...  25 us
    ppermute x20, waiting for transfers between devices, exchanged(): terms.append(lax.ppermute(value, (axis, 'ens'), pairs))  19 us
    all_to_all x1, blocking collectives, per_device(): obs = lax.all_to_all(obs, ('lat_0', 'lon'), 0, 0, tiled=True)  17 us
    ppermute x6, starting transfers between devices, moved(): return lax.ppermute(value, axes, [(i, (i + by) % n) for i in range(n)])  10.8 us
    ppermute x2, waiting for transfers between devices, reduced(): value = total + lax.ppermute(total, 'ens', [(0, 1)])  6.89 us
    unnamed x16, local copies, waits for them, and re-layouts  4.87 us
    ppermute x3, starting transfers between devices, per_device(): lax.ppermute(obs, 'lat_1', [(i, i ^ m) for i in range(4)])  3.95 us
  transfers between devices with their start and end apart: 34, of which 16 were waited for; matrix products, arithmetic and copies ran while one was open for 0% of the time, Pallas kernels for 1%

profile of v1, /device:TPU:1, one launch (start us, length us, event | category | flops | bytes accessed | tf_op | source)
XLA Modules:
  0.0 164.8 jit_solution(3993805257303514877)
XLA Ops:
  0.0 3.2 %collective-permute-start = (f32[1024,128]{1,0:T(8,128)}, f32[1024,128]{1,0:T(8,128)S(1)}, u32[]{:S(2)}, u32[]{:S(2)}) collective-permute-start(f32[1024,128]{1,0:T(8,128)} %bitcast.25), channel_id=1, source_target_pairs={{0,1},{1,0},{2,3},{3,2},{4,5},{5,4},{6,7},{7,6},{8,9},{9,8},{10,11... | collective-permute-start | bytes 1572872 | tf_op jit(solution)/shard_map/ppermute | solution.py:377
  9.3 3.3 %collective-permute-start.2 = (f32[1048,128]{1,0:T(8,128)S(1)}, f32[1048,128]{1,0:T(8,128)S(1)}, u32[]{:S(2)}, u32[]{:S(2)}) collective-permute-start(f32[1048,128]{1,0:T(8,128)S(1)} %get-tuple-element.21.own), channel_id=1, source_target_pairs={{0,240},{16,0},{32,16},{48,32},{64,48},{80,64},{96,80},{112,96},{1... | collective-permute-start | bytes 1609736 | tf_op jit(solution)/shard_map/ppermute | solution.py:382
  12.5 5.1 %collective-permute-start.4 = (f32[216,128]{1,0:T(8,128)S(1)}, f32[216,128]{1,0:T(8,128)S(1)}, u32[]{:S(2)}, u32[]{:S(2)}) collective-permute-start(f32[216,128]{1,0:T(8,128)S(1)} %get-tuple-element.23), channel_id=1, source_target_pairs={{0,224},{16,240},{32,0},{48,16},{64,32},{80,48},{96,64},{112,80},{... | collective-permute-start | bytes 331784 | tf_op jit(solution)/shard_map/ppermute | solution.py:382
  17.6 17.0 %all_to_all.11 = f32[32,1,128]{2,1,0:T(1,128)S(1)} all-to-all(f32[32,1,128]{2,1,0:T(1,128)S(1)} %bitcast.34), channel_id=1, replica_groups=mesh['lat_0'=4,'lat_1'=4,'lon'=8,'ens'=2] {'lat_0','lon'}, dimensions={0} | all-to-all | bytes 32768 | tf_op jit(solution)/shard_map/all_to_all | solution.py:433
  37.2 3.0 %collective-permute-start.9 = (f32[32,128]{1,0:T(8,128)S(1)}, f32[32,128]{1,0:T(8,128)S(1)}, u32[]{:S(2)}, u32[]{:S(2)}) collective-permute-start(f32[32,128]{1,0:T(8,128)S(1)} %bitcast.30), channel_id=1, source_target_pairs={{0,48},{16,32},{32,16},{48,0},{1,49},{17,33},{33,17},{49,1},{2,50}... | collective-permute-start | bytes 49160 | tf_op jit(solution)/shard_map/ppermute | solution.py:434
  41.6 2.8 %collective-permute-done.8.part2 = f32[32,128]{1,0:T(8,128)S(1)} collective-permute-done((f32[32,128]{1,0:T(8,128)S(1)}, f32[32,128]{1,0:T(8,128)S(1)}, u32[]{:S(2)}, u32[]{:S(2)}) %collective-permute-start.8) | collective-permute-done | bytes 16416 | tf_op jit(solution)/shard_map/ppermute | solution.py:434
  45.9 5.3 %shard_map.68 = (f32[28,112,128]{2,1,0:T(8,128)S(1)}, f32[28,112,128]{2,1,0:T(8,128)S(1)}, f32[128,128]{1,0:T(8,128)S(1)}, f32[72,128]{1,0:T(8,128)S(1)}) custom-call(s32[3]{0:T(128)S(1)} %pad_add_fusion.pos, f32[1048,128]{1,0:T(8,128)S(1)} %get-tuple-element.21.own, f32[1048,128]{1,0:T(8,128)S(1)} %collective-permute-done.1.m1, ...), custom_call_target="tpu_custom_call" | custom-call | tf_op jit(solution)/shard_map/pallas_call | solution.py:407
  52.5 5.1 %collective-permute-done.10 = f32[72,128]{1,0:T(8,128)S(1)} collective-permute-done((f32[72,128]{1,0:T(8,128)S(1)}, f32[72,128]{1,0:T(8,128)S(1)}, u32[]{:S(2)}, u32[]{:S(2)}) %collective-permute-start.10) | collective-permute-done | bytes 36896 | tf_op jit(solution)/shard_map/ppermute | solution.py:399
  60.1 3.1 %collective-permute-start.12 = (f32[72,128]{1,0:T(8,128)S(1)}, f32[72,128]{1,0:T(8,128)S(1)}, u32[]{:S(2)}, u32[]{:S(2)}) collective-permute-start(f32[72,128]{1,0:T(8,128)S(1)} %add.70), channel_id=1, source_target_pairs={{1,129},{65,193},{129,1},{193,65},{3,131},{67,195},{131,3},{195,67... | collective-permute-start | bytes 110600 | tf_op jit(solution)/shard_map/ppermute | solution.py:392
  63.2 3.4 %collective-permute-start.11 = (f32[72,128]{1,0:T(8,128)S(1)}, f32[72,128]{1,0:T(8,128)S(1)}, u32[]{:S(2)}, u32[]{:S(2)}) collective-permute-start(f32[72,128]{1,0:T(8,128)S(1)} %add.70), channel_id=1, source_target_pairs={{1,65},{65,1},{129,193},{193,129},{3,67},{67,3},{131,195},{195,131... | collective-permute-start | bytes 110600 | tf_op jit(solution)/shard_map/ppermute | solution.py:392
  70.3 3.2 %collective-permute-start.15 = (f32[72,128]{1,0:T(8,128)S(1)}, f32[72,128]{1,0:T(8,128)S(1)}, u32[]{:S(2)}, u32[]{:S(2)}) collective-permute-start(f32[72,128]{1,0:T(8,128)S(1)} %add_add_fusion.5), channel_id=1, source_target_pairs={{1,33},{17,49},{33,1},{49,17},{3,35},{19,51},{35,3},{51,19},{5,37}... | collective-permute-start | bytes 110600 | tf_op jit(solution)/shard_map/ppermute | solution.py:392
  73.5 3.4 %collective-permute-start.14 = (f32[72,128]{1,0:T(8,128)S(1)}, f32[72,128]{1,0:T(8,128)S(1)}, u32[]{:S(2)}, u32[]{:S(2)}) collective-permute-start(f32[72,128]{1,0:T(8,128)S(1)} %add_add_fusion.5), channel_id=1, source_target_pairs={{1,17},{17,1},{33,49},{49,33},{3,19},{19,3},{35,51},{51,35},{5,21}... | collective-permute-start | bytes 110600 | tf_op jit(solution)/shard_map/ppermute | solution.py:392
  80.2 2.8 %collective-permute-done.17 = f32[72,128]{1,0:T(8,128)S(1)} collective-permute-done((f32[72,128]{1,0:T(8,128)S(1)}, f32[72,128]{1,0:T(8,128)S(1)}, u32[]{:S(2)}, u32[]{:S(2)}) %collective-permute-start.17) | collective-permute-done | bytes 36896 | tf_op jit(solution)/shard_map/ppermute | solution.py:392
  83.0 4.7 %collective-permute-start.20 = (f32[72,128]{1,0:T(8,128)S(1)}, f32[72,128]{1,0:T(8,128)S(1)}, u32[]{:S(2)}, u32[]{:S(2)}) collective-permute-start(f32[72,128]{1,0:T(8,128)S(1)} %add.77), channel_id=1, source_target_pairs={{1,13},{3,15},{5,9},{7,11},{9,5},{11,7},{13,1},{15,3},{17,29},{19,... | collective-permute-start | bytes 110600 | tf_op jit(solution)/shard_map/ppermute | solution.py:392
  87.7 4.8 %collective-permute-start.19 = (f32[72,128]{1,0:T(8,128)S(1)}, f32[72,128]{1,0:T(8,128)S(1)}, u32[]{:S(2)}, u32[]{:S(2)}) collective-permute-start(f32[72,128]{1,0:T(8,128)S(1)} %add.77), channel_id=1, source_target_pairs={{1,9},{3,11},{5,13},{7,15},{9,1},{11,3},{13,5},{15,7},{17,25},{19,... | collective-permute-start | bytes 110600 | tf_op jit(solution)/shard_map/ppermute | solution.py:392
  100.3 10.9 %shard_map.69 = (f32[128,128]{1,0:T(8,128)S(1)}, f32[72,128]{1,0:T(8,128)S(1)}) custom-call(s32[3]{0:T(128)S(1)} %pad_add_fusion.pos, f32[72,128]{1,0:T(8,128)S(1)} %add_add_fusion.3.mine, f32[72,128]{1,0:T(8,128)S(1)} %collective-permute-done.21.other, f32[28,112,128]{2,1,0:T(8,128)S(1)} %get-tuple-element.30.fr, f32[28,112,128]{2,1,0:T(8,128)S(1)} %get-tuple-element.31.fo, ...), custom_call_target="tpu_custom_call" | custom-call | tf_op jit(solution)/shard_map/pallas_call | solution.py:407
  114.3 2.8 %collective-permute-start.25 = (f32[72,128]{1,0:T(8,128)S(1)}, f32[72,128]{1,0:T(8,128)S(1)}, u32[]{:S(2)}, u32[]{:S(2)}) collective-permute-start(f32[72,128]{1,0:T(8,128)S(1)} %add.81), channel_id=1, source_target_pairs={{1,193},{65,129},{129,65},{193,1},{3,195},{67,131},{131,67},{195,3... | collective-permute-start | bytes 110600 | tf_op jit(solution)/shard_map/ppermute | solution.py:392
  117.1 4.3 %collective-permute-start.24 = (f32[72,128]{1,0:T(8,128)S(1)}, f32[72,128]{1,0:T(8,128)S(1)}, u32[]{:S(2)}, u32[]{:S(2)}) collective-permute-start(f32[72,128]{1,0:T(8,128)S(1)} %add.81), channel_id=1, source_target_pairs={{1,129},{65,193},{129,1},{193,65},{3,131},{67,195},{131,3},{195,67... | collective-permute-start | bytes 110600 | tf_op jit(solution)/shard_map/ppermute | solution.py:392
  128.7 3.6 %collective-permute-start.27 = (f32[72,128]{1,0:T(8,128)S(1)}, f32[72,128]{1,0:T(8,128)S(1)}, u32[]{:S(2)}, u32[]{:S(2)}) collective-permute-start(f32[72,128]{1,0:T(8,128)S(1)} %add_add_fusion.2), channel_id=1, source_target_pairs={{1,33},{17,49},{33,1},{49,17},{3,35},{19,51},{35,3},{51,19},{5,37}... | collective-permute-start | bytes 110600 | tf_op jit(solution)/shard_map/ppermute | solution.py:392
  141.8 5.5 %collective-permute-start.32 = (f32[72,128]{1,0:T(8,128)S(1)}, f32[72,128]{1,0:T(8,128)S(1)}, u32[]{:S(2)}, u32[]{:S(2)}) collective-permute-start(f32[72,128]{1,0:T(8,128)S(1)} %add.88), channel_id=1, source_target_pairs={{1,13},{3,15},{5,9},{7,11},{9,5},{11,7},{13,1},{15,3},{17,29},{19,... | collective-permute-start | bytes 110600 | tf_op jit(solution)/shard_map/ppermute | solution.py:392
  147.3 3.1 %collective-permute-start.31 = (f32[72,128]{1,0:T(8,128)S(1)}, f32[72,128]{1,0:T(8,128)S(1)}, u32[]{:S(2)}, u32[]{:S(2)}) collective-permute-start(f32[72,128]{1,0:T(8,128)S(1)} %add.88), channel_id=1, source_target_pairs={{1,9},{3,11},{5,13},{7,15},{9,1},{11,3},{13,5},{15,7},{17,25},{19,... | collective-permute-start | bytes 110600 | tf_op jit(solution)/shard_map/ppermute | solution.py:392
  150.4 2.8 %collective-permute-start.30 = (f32[72,128]{1,0:T(8,128)S(1)}, f32[72,128]{1,0:T(8,128)S(1)}, u32[]{:S(2)}, u32[]{:S(2)}) collective-permute-start(f32[72,128]{1,0:T(8,128)S(1)} %add.88), channel_id=1, source_target_pairs={{1,5},{3,7},{5,1},{7,3},{9,13},{11,15},{13,9},{15,11},{17,21},{19,... | collective-permute-start | bytes 110600 | tf_op jit(solution)/shard_map/ppermute | solution.py:392
  153.2 2.8 %collective-permute-done.31 = f32[72,128]{1,0:T(8,128)S(1)} collective-permute-done((f32[72,128]{1,0:T(8,128)S(1)}, f32[72,128]{1,0:T(8,128)S(1)}, u32[]{:S(2)}, u32[]{:S(2)}) %collective-permute-start.31) | collective-permute-done | bytes 36896 | tf_op jit(solution)/shard_map/ppermute | solution.py:392
  158.6 6.2 %shard_map.70 = f32[1024,128]{1,0:T(8,128)} custom-call(s32[3]{0:T(128)S(1)} %pad_add_fusion.pos, f32[72,128]{1,0:T(8,128)S(1)} %add_add_fusion.mine, f32[72,128]{1,0:T(8,128)S(1)} %collective-permute-done.33.other, f32[128,128]{1,0:T(8,128)S(1)} %get-tuple-element.34.k1, f32[1024,128]{1,0:T(8,128)S(1)} %bitcast.28, ...), custom_call_target="tpu_custom_call" | custom-call | tf_op jit(solution)/shard_map/pallas_call | solution.py:407
  (79 shorter events, 52.3 us)
Async XLA Ops:
  0.0 7.3 %collective-permute-start = (f32[1024,128]{1,0:T(8,128)}, f32[1024,128]{1,0:T(8,128)S(1)}, u32[]{:S(2)}, u32[]{:S(2)}) collective-permute-start(f32[1024,128]{1,0:T(8,128)} %bitcast.25), channel_id=1, source_target_pairs={{0,1},{1,0},{2,3},{3,2},{4,5},{5,4},{6,7},{7,6},{8,9},{9,8},{10,11... | collective-permute-start | bytes 1572872 | tf_op jit(solution)/shard_map/ppermute | solution.py:377
  9.3 25.4 %collective-permute-start.2 = (f32[1048,128]{1,0:T(8,128)S(1)}, f32[1048,128]{1,0:T(8,128)S(1)}, u32[]{:S(2)}, u32[]{:S(2)}) collective-permute-start(f32[1048,128]{1,0:T(8,128)S(1)} %get-tuple-element.21.own), channel_id=1, source_target_pairs={{0,240},{16,0},{32,16},{48,32},{64,48},{80,64},{96,80},{112,96},{1... | collective-permute-start | bytes 1609736 | tf_op jit(solution)/shard_map/ppermute | solution.py:382
  12.5 22.1 %collective-permute-start.1 = (f32[1048,128]{1,0:T(8,128)S(1)}, f32[1048,128]{1,0:T(8,128)S(1)}, u32[]{:S(2)}, u32[]{:S(2)}) collective-permute-start(f32[1048,128]{1,0:T(8,128)S(1)} %get-tuple-element.21.own), channel_id=1, source_target_pairs={{0,16},{16,32},{32,48},{48,64},{64,80},{80,96},{96,112},{112,128},... | collective-permute-start | bytes 1609736 | tf_op jit(solution)/shard_map/ppermute | solution.py:382
  12.5 22.1 %collective-permute-start.3 = (f32[216,128]{1,0:T(8,128)S(1)}, f32[216,128]{1,0:T(8,128)S(1)}, u32[]{:S(2)}, u32[]{:S(2)}) collective-permute-start(f32[216,128]{1,0:T(8,128)S(1)} %get-tuple-element.22), channel_id=1, source_target_pairs={{0,32},{16,48},{32,64},{48,80},{64,96},{80,112},{96,128},{112,144}... | collective-permute-start | bytes 331784 | tf_op jit(solution)/shard_map/ppermute | solution.py:382
  12.5 22.1 %collective-permute-start.4 = (f32[216,128]{1,0:T(8,128)S(1)}, f32[216,128]{1,0:T(8,128)S(1)}, u32[]{:S(2)}, u32[]{:S(2)}) collective-permute-start(f32[216,128]{1,0:T(8,128)S(1)} %get-tuple-element.23), channel_id=1, source_target_pairs={{0,224},{16,240},{32,0},{48,16},{64,32},{80,48},{96,64},{112,80},{... | collective-permute-start | bytes 331784 | tf_op jit(solution)/shard_map/ppermute | solution.py:382
  34.7 11.2 %collective-permute-start.5 = (f32[696,128]{1,0:T(8,128)S(1)}, f32[696,128]{1,0:T(8,128)S(1)}, u32[]{:S(2)}, u32[]{:S(2)}) collective-permute-start(f32[696,128]{1,0:T(8,128)S(1)} %get-tuple-element.25), channel_id=1, source_target_pairs={{0,1},{1,2},{2,3},{3,4},{4,5},{5,6},{6,7},{7,8},{8,9},{9,10},{10,1... | collective-permute-start | bytes 1069064 | tf_op jit(solution)/shard_map/ppermute | solution.py:382
  37.2 8.7 %collective-permute-start.6 = (f32[696,128]{1,0:T(8,128)S(1)}, f32[696,128]{1,0:T(8,128)S(1)}, u32[]{:S(2)}, u32[]{:S(2)}) collective-permute-start(f32[696,128]{1,0:T(8,128)S(1)} %get-tuple-element.26), channel_id=1, source_target_pairs={{0,15},{1,0},{2,1},{3,2},{4,3},{5,4},{6,5},{7,6},{8,7},{9,8},{10,9... | collective-permute-start | bytes 1069064 | tf_op jit(solution)/shard_map/ppermute | solution.py:382
  51.2 6.4 %collective-permute-start.10 = (f32[72,128]{1,0:T(8,128)S(1)}, f32[72,128]{1,0:T(8,128)S(1)}, u32[]{:S(2)}, u32[]{:S(2)}) collective-permute-start(f32[72,128]{1,0:T(8,128)S(1)} %get-tuple-element.29), channel_id=1, source_target_pairs={{0,1},{2,3},{4,5},{6,7},{8,9},{10,11},{12,13},{14,15},{16,17},{18,... | collective-permute-start | bytes 110600 | tf_op jit(solution)/shard_map/ppermute | solution.py:399
  57.6 9.0 %collective-permute-start.13 = (f32[72,128]{1,0:T(8,128)S(1)}, f32[72,128]{1,0:T(8,128)S(1)}, u32[]{:S(2)}, u32[]{:S(2)}) collective-permute-start(f32[72,128]{1,0:T(8,128)S(1)} %add.70), channel_id=1, source_target_pairs={{1,193},{65,129},{129,65},{193,1},{3,195},{67,131},{131,67},{195,3... | collective-permute-start | bytes 110600 | tf_op jit(solution)/shard_map/ppermute | solution.py:392
  60.1 6.6 %collective-permute-start.12 = (f32[72,128]{1,0:T(8,128)S(1)}, f32[72,128]{1,0:T(8,128)S(1)}, u32[]{:S(2)}, u32[]{:S(2)}) collective-permute-start(f32[72,128]{1,0:T(8,128)S(1)} %add.70), channel_id=1, source_target_pairs={{1,129},{65,193},{129,1},{193,65},{3,131},{67,195},{131,3},{195,67... | collective-permute-start | bytes 110600 | tf_op jit(solution)/shard_map/ppermute | solution.py:392
  63.2 4.7 %collective-permute-start.11 = (f32[72,128]{1,0:T(8,128)S(1)}, f32[72,128]{1,0:T(8,128)S(1)}, u32[]{:S(2)}, u32[]{:S(2)}) collective-permute-start(f32[72,128]{1,0:T(8,128)S(1)} %add.70), channel_id=1, source_target_pairs={{1,65},{65,1},{129,193},{193,129},{3,67},{67,3},{131,195},{195,131... | collective-permute-start | bytes 110600 | tf_op jit(solution)/shard_map/ppermute | solution.py:392
  67.9 9.0 %collective-permute-start.16 = (f32[72,128]{1,0:T(8,128)S(1)}, f32[72,128]{1,0:T(8,128)S(1)}, u32[]{:S(2)}, u32[]{:S(2)}) collective-permute-start(f32[72,128]{1,0:T(8,128)S(1)} %add_add_fusion.5), channel_id=1, source_target_pairs={{1,49},{17,33},{33,17},{49,1},{3,51},{19,35},{35,19},{51,3},{5,53}... | collective-permute-start | bytes 110600 | tf_op jit(solution)/shard_map/ppermute | solution.py:392
  70.3 6.7 %collective-permute-start.15 = (f32[72,128]{1,0:T(8,128)S(1)}, f32[72,128]{1,0:T(8,128)S(1)}, u32[]{:S(2)}, u32[]{:S(2)}) collective-permute-start(f32[72,128]{1,0:T(8,128)S(1)} %add_add_fusion.5), channel_id=1, source_target_pairs={{1,33},{17,49},{33,1},{49,17},{3,35},{19,51},{35,3},{51,19},{5,37}... | collective-permute-start | bytes 110600 | tf_op jit(solution)/shard_map/ppermute | solution.py:392
  73.5 4.8 %collective-permute-start.14 = (f32[72,128]{1,0:T(8,128)S(1)}, f32[72,128]{1,0:T(8,128)S(1)}, u32[]{:S(2)}, u32[]{:S(2)}) collective-permute-start(f32[72,128]{1,0:T(8,128)S(1)} %add_add_fusion.5), channel_id=1, source_target_pairs={{1,17},{17,1},{33,49},{49,33},{3,19},{19,3},{35,51},{51,35},{5,21}... | collective-permute-start | bytes 110600 | tf_op jit(solution)/shard_map/ppermute | solution.py:392
  83.0 11.5 %collective-permute-start.20 = (f32[72,128]{1,0:T(8,128)S(1)}, f32[72,128]{1,0:T(8,128)S(1)}, u32[]{:S(2)}, u32[]{:S(2)}) collective-permute-start(f32[72,128]{1,0:T(8,128)S(1)} %add.77), channel_id=1, source_target_pairs={{1,13},{3,15},{5,9},{7,11},{9,5},{11,7},{13,1},{15,3},{17,29},{19,... | collective-permute-start | bytes 110600 | tf_op jit(solution)/shard_map/ppermute | solution.py:392
  87.7 8.6 %collective-permute-start.19 = (f32[72,128]{1,0:T(8,128)S(1)}, f32[72,128]{1,0:T(8,128)S(1)}, u32[]{:S(2)}, u32[]{:S(2)}) collective-permute-start(f32[72,128]{1,0:T(8,128)S(1)} %add.77), channel_id=1, source_target_pairs={{1,9},{3,11},{5,13},{7,15},{9,1},{11,3},{13,5},{15,7},{17,25},{19,... | collective-permute-start | bytes 110600 | tf_op jit(solution)/shard_map/ppermute | solution.py:392
  92.6 5.6 %collective-permute-start.18 = (f32[72,128]{1,0:T(8,128)S(1)}, f32[72,128]{1,0:T(8,128)S(1)}, u32[]{:S(2)}, u32[]{:S(2)}) collective-permute-start(f32[72,128]{1,0:T(8,128)S(1)} %add.77), channel_id=1, source_target_pairs={{1,5},{3,7},{5,1},{7,3},{9,13},{11,15},{13,9},{15,11},{17,21},{19,... | collective-permute-start | bytes 110600 | tf_op jit(solution)/shard_map/ppermute | solution.py:392
  114.3 9.0 %collective-permute-start.25 = (f32[72,128]{1,0:T(8,128)S(1)}, f32[72,128]{1,0:T(8,128)S(1)}, u32[]{:S(2)}, u32[]{:S(2)}) collective-permute-start(f32[72,128]{1,0:T(8,128)S(1)} %add.81), channel_id=1, source_target_pairs={{1,193},{65,129},{129,65},{193,1},{3,195},{67,131},{131,67},{195,3... | collective-permute-start | bytes 110600 | tf_op jit(solution)/shard_map/ppermute | solution.py:392
  117.1 6.2 %collective-permute-start.24 = (f32[72,128]{1,0:T(8,128)S(1)}, f32[72,128]{1,0:T(8,128)S(1)}, u32[]{:S(2)}, u32[]{:S(2)}) collective-permute-start(f32[72,128]{1,0:T(8,128)S(1)} %add.81), channel_id=1, source_target_pairs={{1,129},{65,193},{129,1},{193,65},{3,131},{67,195},{131,3},{195,67... | collective-permute-start | bytes 110600 | tf_op jit(solution)/shard_map/ppermute | solution.py:392
  126.1 9.0 %collective-permute-start.28 = (f32[72,128]{1,0:T(8,128)S(1)}, f32[72,128]{1,0:T(8,128)S(1)}, u32[]{:S(2)}, u32[]{:S(2)}) collective-permute-start(f32[72,128]{1,0:T(8,128)S(1)} %add_add_fusion.2), channel_id=1, source_target_pairs={{1,49},{17,33},{33,17},{49,1},{3,51},{19,35},{35,19},{51,3},{5,53}... | collective-permute-start | bytes 110600 | tf_op jit(solution)/shard_map/ppermute | solution.py:392
  128.7 6.4 %collective-permute-start.27 = (f32[72,128]{1,0:T(8,128)S(1)}, f32[72,128]{1,0:T(8,128)S(1)}, u32[]{:S(2)}, u32[]{:S(2)}) collective-permute-start(f32[72,128]{1,0:T(8,128)S(1)} %add_add_fusion.2), channel_id=1, source_target_pairs={{1,33},{17,49},{33,1},{49,17},{3,35},{19,51},{35,3},{51,19},{5,37}... | collective-permute-start | bytes 110600 | tf_op jit(solution)/shard_map/ppermute | solution.py:392
  141.8 11.4 %collective-permute-start.32 = (f32[72,128]{1,0:T(8,128)S(1)}, f32[72,128]{1,0:T(8,128)S(1)}, u32[]{:S(2)}, u32[]{:S(2)}) collective-permute-start(f32[72,128]{1,0:T(8,128)S(1)} %add.88), channel_id=1, source_target_pairs={{1,13},{3,15},{5,9},{7,11},{9,5},{11,7},{13,1},{15,3},{17,29},{19,... | collective-permute-start | bytes 110600 | tf_op jit(solution)/shard_map/ppermute | solution.py:392
  147.3 8.7 %collective-permute-start.31 = (f32[72,128]{1,0:T(8,128)S(1)}, f32[72,128]{1,0:T(8,128)S(1)}, u32[]{:S(2)}, u32[]{:S(2)}) collective-permute-start(f32[72,128]{1,0:T(8,128)S(1)} %add.88), channel_id=1, source_target_pairs={{1,9},{3,11},{5,13},{7,15},{9,1},{11,3},{13,5},{15,7},{17,25},{19,... | collective-permute-start | bytes 110600 | tf_op jit(solution)/shard_map/ppermute | solution.py:392
  150.4 6.0 %collective-permute-start.30 = (f32[72,128]{1,0:T(8,128)S(1)}, f32[72,128]{1,0:T(8,128)S(1)}, u32[]{:S(2)}, u32[]{:S(2)}) collective-permute-start(f32[72,128]{1,0:T(8,128)S(1)} %add.88), channel_id=1, source_target_pairs={{1,5},{3,7},{5,1},{7,3},{9,13},{11,15},{13,9},{15,11},{17,21},{19,... | collective-permute-start | bytes 110600 | tf_op jit(solution)/shard_map/ppermute | solution.py:392
  (18 other events, 138.2 us)
